TPU v7x, 256 devices: a whole 4x4x8 slice. The times are simulated.
256 devices in a mesh: ga: 16 (over z_lo, y), pair: 16 (over z_hi, x, core).
Axes of the slice: x: 4, y: 4, z: 8 (z_hi: 2, z_lo: 4; z = z_hi * 4 + z_lo), core: 2. Of those that a mesh axis runs over, the one named last changes fastest.
Arguments:
- val_density: bfloat16 [256, 3, 2, 8192], P('pair', None, None, 'ga'), may hold values from -0.0625 to 0.0625
- con_density: bfloat16 [576, 3, 2, 8192], P('ga', None, None, 'pair'), may hold values from -6 to 6
- screened: bfloat16 [3, 2, 8192, 8192], P(None, None, 'ga', 'pair'), may hold values from -0.0625 to 0.0625
- coulomb: float32 [3, 8192], P(None, 'ga'), may hold values from 0.2 to 2
- trans_here: bfloat16 [384, 2, 8192], P('pair', None, 'ga'), may hold values from -6 to 6
- trans_there: bfloat16 [384, 3, 2, 8192], P('pair', None, None, 'ga'), may hold values from -0.0625 to 0.0625
- shift_map: int32 [3, 8192], P(None, 'pair'), may hold values from 0 to 8191, as said below
- ordering: int32 [384], replicated, may hold values from 0 to 383, each once
Outputs:
- kernel: float32 [3, 2, 384, 384], P(None, None, 'pair', 'ga')
Inputs may be any that keep to these rules, and one draw needn't show every extreme that they name: `shift_map`: each aligned block of 128 entries of a row is a permutation of that block's own G-vector indices.
All inputs are finite; a program needn't handle non-finite values.
Results may differ from a plain program's by a relative error of at most 0.0003.
Values may be sent and summed in bfloat16 or wider, within the bound.
A program may use at most 64 MiB of HBM per device.

v0:
```python
import jax
import jax.numpy as jnp
from jax import lax
from jax.sharding import PartitionSpec as P

NV = 16
NC = 24
GBLK = 128
NT = 384
F32 = jnp.float32
BF16 = jnp.bfloat16


def two_terms(values):
    high = lax.reduce_precision(values, exponent_bits=8, mantissa_bits=7)
    low = lax.reduce_precision(values - high, exponent_bits=8, mantissa_bits=7)
    return (high.astype(BF16), low.astype(BF16))


def on_device(
    val_density, con_density, screened, coulomb, trans_here, trans_there, shift_map, ordering
):
    con_count, points, _, slab_cols = con_density.shape
    blocks = slab_cols // GBLK
    pairs = lax.axis_size("pair")
    slabs = lax.axis_size("ga")
    whole_con = lax.all_gather(con_density, "ga", axis=0, tiled=True)
    whole_val = lax.all_gather(val_density, "pair", axis=0, tiled=True)
    whole_here = lax.all_gather(trans_here, "pair", axis=0, tiled=True)
    within = (shift_map % GBLK).reshape(points, blocks, GBLK)
    onehot = (
        within[:, :, :, None] == jnp.arange(GBLK, dtype=jnp.int32)[None, None, None, :]
    ).astype(BF16)

    def mul(spec, left, right):
        return jnp.einsum(spec, left, right, preferred_element_type=F32)

    rows_re = mul("akg,kgh->kah", whole_val[:, :, 0], screened[:, 0]) - mul(
        "akg,kgh->kah", whole_val[:, :, 1], screened[:, 1]
    )
    rows_im = mul("akg,kgh->kah", whole_val[:, :, 0], screened[:, 1]) + mul(
        "akg,kgh->kah", whole_val[:, :, 1], screened[:, 0]
    )
    shape = (points, NV * NV, blocks, GBLK)

    def unshift(term):
        moved = mul("kang,kngh->kanh", term.reshape(shape), onehot).astype(BF16)
        return moved.reshape(points, NV * NV, slab_cols)

    real = [unshift(term) for term in two_terms(rows_re)]
    imag = [unshift(term) for term in two_terms(rows_im)]
    left_re = jnp.concatenate([real[0], -imag[0], real[1], -imag[1]], axis=2)
    left_im = jnp.concatenate([imag[0], real[0], imag[1], real[1]], axis=2)
    con_rows = jnp.transpose(whole_con, (1, 0, 2, 3)).reshape(points, NC * NC, 2 * slab_cols)
    con_twice = jnp.concatenate([con_rows, con_rows], axis=2)
    direct = jnp.stack(
        [mul("kax,kbx->kab", left_re, con_twice), mul("kax,kbx->kab", left_im, con_twice)], axis=1
    )
    direct = jnp.transpose(direct.reshape(points, 2, NV, NV, NC * NC), (3, 0, 1, 2, 4))
    direct = lax.psum_scatter(direct, "pair", scatter_dimension=0, tiled=True)[0]
    direct = jnp.transpose(direct.reshape(points, 2, NV, NC, NC), (2, 3, 0, 1, 4)).reshape(
        NT, points, 2, NC
    )
    weighted = trans_there.astype(F32) * coulomb[None, :, None, :]
    high = lax.Precision.HIGHEST
    here = whole_here.astype(F32)
    exch_re = jnp.einsum("tg,skg->tks", here[:, 0], weighted[:, :, 0], precision=high) - jnp.einsum(
        "tg,skg->tks", here[:, 1], weighted[:, :, 1], precision=high
    )
    exch_im = jnp.einsum("tg,skg->tks", here[:, 0], weighted[:, :, 1], precision=high) + jnp.einsum(
        "tg,skg->tks", here[:, 1], weighted[:, :, 0], precision=high
    )
    natural = 2.0 * jnp.stack([exch_re, exch_im], axis=2) - direct
    rows = natural[ordering]
    rows = lax.all_to_all(
        rows.reshape(pairs, NT // pairs, points, 2, NC), "pair", split_axis=0, concat_axis=0
    )
    cols = jnp.transpose(rows, (0, 4, 2, 3, 1)).reshape(NT, points * 2 * (NT // pairs))
    cols = cols[ordering]
    cols = lax.psum_scatter(cols, "ga", scatter_dimension=0, tiled=True)
    cols = cols.reshape(NT // slabs, points, 2, NT // pairs)
    return jnp.transpose(cols, (1, 2, 3, 0))


def solution(mesh):
    in_specs = (
        P("pair", None, None, "ga"),
        P("ga", None, None, "pair"),
        P(None, None, "ga", "pair"),
        P(None, "ga"),
        P("pair", None, "ga"),
        P("pair", None, None, "ga"),
        P(None, "pair"),
        P(),
    )
    out_specs = P(None, None, "pair", "ga")
    return jax.shard_map(
        on_device, mesh=mesh, in_specs=in_specs, out_specs=out_specs, check_vma=False
    )
```

profile of v0, /device:TPU:2, one launch (start us, length us, event | category | flops | bytes accessed | tf_op | source)
XLA Modules:
  0.0 404.5 jit_solution(9876181623509086774)
XLA Ops:
  6.5 0.0 all-gather.3.cloned.1.call-start
  6.5 1.7 copy.57
  8.2 0.0 all-gather.3.cloned.1.call-update
  8.3 0.0 all-gather.5.cloned.1.call-start
  8.3 0.7 all-gather.5.cloned.1.call-update
  9.0 0.0 reduce-scatter.3.cloned.1.call-start
  9.1 0.7 add_select_fusion
  9.8 62.1 %all-gather.3.cloned.1.call-done = bf16[256,3,2,512]{3,0,1,2:T(8,128)(2,1)} async-done(((bf16[16,3,2,512]{3,0,1,2:T(8,128)(2,1)}), bf16[256,3,2,512]{3,0,1,2:T(8,128)(2,1)}) %all-gather.3.cloned.1.call-update) | async-done | bytes 1572880 | tf_op jit(solution)/shard_map/all_gather | solution.py:28
  71.9 2.2 fusion.22
  74.1 0.0 copy-done
  74.1 2.7 fusion.42
  76.8 1.3 convolution_convert_fusion.1
  78.1 2.3 copy.67
  80.4 1.9 fusion.20
  82.3 1.5 fusion.43
  83.8 0.4 convolution_convert_fusion
  84.2 0.3 copy.65
  84.5 0.0 copy-start.2
  84.5 0.5 copy-done.6
  84.9 0.4 convolution_convert_fusion.3
  85.3 1.2 copy.66
  86.6 0.4 convolution_convert_fusion.2
  86.9 0.3 copy.62
  87.3 1.1 neg.7
  88.4 1.0 neg.6
  89.4 66.7 %all-gather.5.cloned.1.call-done = bf16[576,3,2,512]{3,2,1,0:T(2,128)(2,1)} async-done(((bf16[36,3,2,512]{3,2,1,0:T(2,128)(2,1)}), bf16[576,3,2,512]{3,2,1,0:T(2,128)(2,1)}) %all-gather.5.cloned.1.call-update) | async-done | bytes 3538960 | tf_op jit(solution)/shard_map/all_gather | solution.py:27
  156.1 6.2 %copy.68 = bf16[3,576,2,512]{3,2,1,0:T(2,128)(2,1)} copy(bf16[3,576,2,512]{3,2,0,1:T(2,128)(2,1)} %bitcast.118) | data formatting | bytes 7077888 | tf_op jit(solution)/shard_map/transpose | solution.py:54
  162.4 7.8 %reshape.54 = bf16[3,576,1024]{2,1,0:T(8,128)(2,1)S(1)} reshape(bf16[3,576,2,512]{3,2,1,0:T(2,128)(2,1)} %copy.68) | data formatting | bytes 7077888 | tf_op jit(solution)/shard_map/reshape | solution.py:54
  170.2 0.5 constant_dynamic-update-slice_fusion.1
  170.7 0.5 constant_dynamic-update-slice_fusion
  171.2 0.6 copy-done.3
  171.8 0.2 copy-done.5
  172.1 6.3 %fusion.8 = f32[3,256,576]{2,1,0:T(8,128)S(1)} fusion(bf16[3,576,2048]{2,1,0:T(8,128)(2,1)S(1)} %constant_dynamic-update-slice_fusion, bf16[3,256,512]{2,1,0:T(8,128)(2,1)} %copy.67, bf16[3,256,512]{2,1,0:T(8,128)(2,1)S(1)} %copy-done.3, bf16[3,256,512]{2,1,0:T(8,128)(2,1)} %copy.66, bf16[3,256,512]{2,1,0:T(8,128)(2,1)S(1)} %copy-done.5), kind=kOutput, calls=%fused_computation.11 | convolution fusion | flops 1824522240 | bytes 11993088 | tf_op jit(solution)/shard_map/kax,kbx->kab/dot_general | solution.py:36
  178.5 2.6 fusion
  181.1 0.3 maximum_bitcast_fusion
  181.4 3.1 copy.75
  184.4 0.0 reduce-scatter.3.cloned.1.call-update
  184.5 0.0 reduce-scatter.5.cloned.1.call-start
  184.5 0.7 copy-done.13
  185.2 0.0 copy-done.15
  185.3 0.1 copy-done.12
  185.4 26.4 %all_gather.9 = bf16[384,2,512]{2,0,1:T(8,128)(2,1)S(1)} all-gather(bf16[24,2,512]{2,0,1:T(8,128)(2,1)S(1)} %copy.56), channel_id=1, replica_groups=mesh['ga'=16,'pair'=16] {'pair'}, dimensions={0}, use_global_device_ids=true | all-gather | bytes 835584 | tf_op jit(solution)/shard_map/all_gather | solution.py:29
  211.8 0.5 fusion.56
  212.3 0.5 fusion.38
  212.8 0.5 fusion.57
  213.3 0.5 fusion.39
  213.8 70.6 %reduce-scatter.3.cloned.1.call-done = f32[1,3,2,16,576]{4,3,2,1,0:T(8,128)} async-done(((f32[16,3,2,16,576]{4,3,2,1,0:T(8,128)}), f32[1,3,2,16,576]{4,3,2,1,0:T(8,128)}) %reduce-scatter.3.cloned.1.call-update) | async-done | bytes 221200 | tf_op jit(solution)/shard_map/reduce_scatter | solution.py:60
  284.4 1.4 reshape_squeeze.3
  285.8 0.3 copy.84
  286.2 1.1 copy.77
  287.2 3.3 gather_fusion
  290.6 0.1 copy.112
  290.7 0.9 reshape.80
  291.6 13.5 %all_to_all.5 = f32[16,1,3456]{2,1,0:T(1,128)S(1)} all-to-all(f32[16,1,3456]{2,1,0:T(1,128)S(1)} %reshape.80), channel_id=1, replica_groups=mesh['ga'=16,'pair'=16] {'pair'}, dimensions={0} | all-to-all | bytes 442368 | tf_op jit(solution)/shard_map/all_to_all | solution.py:75
  305.1 0.5 broadcast.25
  305.6 1.2 reduce
  306.7 0.7 reshape.81
  307.5 0.1 bitcast_bitcast_fusion
  307.6 0.8 copy.85
  308.4 0.7 reshape.79
  309.1 2.2 gather_fusion.1
  311.3 0.0 reduce-scatter.5.cloned.1.call-update
  311.3 85.2 %reduce-scatter.5.cloned.1.call-done = f32[24,144]{1,0:T(8,128)} async-done(((f32[384,144]{1,0:T(8,128)}), f32[24,144]{1,0:T(8,128)}) %reduce-scatter.5.cloned.1.call-update) | async-done | bytes 13840 | tf_op jit(solution)/shard_map/reduce_scatter | solution.py:80
  396.5 1.5 copy.86
  (30 shorter events, 0.1 us)
Async XLA Ops:
  6.5 67.6 %copy-start = (bf16[3,2,512,512]{3,2,1,0:T(8,128)(2,1)S(1)}, bf16[3,2,512,512]{3,2,1,0:T(8,128)(2,1)}, u32[]{:S(2)}) copy-start(bf16[3,2,512,512]{3,2,1,0:T(8,128)(2,1)} %param.10) | copy-start | bytes 9437188
  6.5 65.3 %all-gather.3.cloned.1.call-start = ((), (), s32[]{:S(2)}) async-start(), calls=%async_computation.3 | async-start | bytes 1671168 | tf_op jit(solution)/shard_map/all_gather | solution.py:28
  8.3 147.9 %all-gather.5.cloned.1.call-start = ((), (), s32[]{:S(2)}) async-start(), calls=%async_computation.4 | async-start | bytes 3760128 | tf_op jit(solution)/shard_map/all_gather | solution.py:27
  9.0 275.4 %reduce-scatter.3.cloned.1.call-start = ((), (), s32[]{:S(2)}) async-start(), calls=%async_computation.5 | async-start | bytes 4177920 | tf_op jit(solution)/shard_map/reduce_scatter | solution.py:60
  80.4 1.9 copy-start.1
  83.8 1.1 copy-start.6
  83.8 2.8 copy-start.7
  84.5 2.7 copy-start.2
  87.2 68.9 %copy-start.4 = (bf16[3,256,512]{2,1,0:T(8,128)(2,1)}, bf16[3,256,512]{2,1,0:T(8,128)(2,1)S(1)}, u32[]{:S(2)}) copy-start(bf16[3,256,512]{2,1,0:T(8,128)(2,1)S(1)} %copy.62) | copy-start | bytes 2359300
  170.7 1.1 copy-start.3
  170.7 1.4 copy-start.5
  172.1 6.4 %copy-start.8 = (bf16[3,256,512]{2,1,0:T(8,128)(2,1)S(1)}, bf16[3,256,512]{2,1,0:T(8,128)(2,1)}, u32[]{:S(2)}) copy-start(bf16[3,256,512]{2,1,0:T(8,128)(2,1)} %copy.67) | copy-start | bytes 2359300
  172.1 6.4 %copy-start.9 = (bf16[3,256,512]{2,1,0:T(8,128)(2,1)S(1)}, bf16[3,256,512]{2,1,0:T(8,128)(2,1)}, u32[]{:S(2)}) copy-start(bf16[3,256,512]{2,1,0:T(8,128)(2,1)} %copy.66) | copy-start | bytes 2359300
  172.1 6.4 %copy-start.10 = (bf16[3,256,512]{2,1,0:T(8,128)(2,1)S(1)}, bf16[3,256,512]{2,1,0:T(8,128)(2,1)}, u32[]{:S(2)}) copy-start(bf16[3,256,512]{2,1,0:T(8,128)(2,1)} %neg.7) | copy-start | bytes 2359300
  172.1 6.4 %copy-start.11 = (bf16[3,256,512]{2,1,0:T(8,128)(2,1)S(1)}, bf16[3,256,512]{2,1,0:T(8,128)(2,1)}, u32[]{:S(2)}) copy-start(bf16[3,256,512]{2,1,0:T(8,128)(2,1)} %neg.6) | copy-start | bytes 2359300
  184.4 0.8 copy-start.13
  184.4 0.8 copy-start.15
  184.4 1.0 copy-start.12
  184.4 1.0 copy-start.14
  184.5 212.1 %reduce-scatter.5.cloned.1.call-start = ((), (), s32[]{:S(2)}) async-start(), calls=%async_computation.6 | async-start | bytes 417792 | tf_op jit(solution)/shard_map/reduce_scatter | solution.py:80
Sparse Core Ops, SparseCore 0:
  10.1 61.7 all-gather.2
  73.7 82.4 all-gather.4
  184.6 99.7 reduce-scatter.2
  311.4 85.0 reduce-scatter.4
where the time goes:
time: 405 us
  waiting for transfers between devices  285 us (70%)
  blocking collectives  39.9 us (10%)
  local copies, waits for them, and re-layouts  39.7 us (10%)
  matrix products  21.6 us (5%)
  between operations  13.5 us (3%)
  other arithmetic  4.33 us (1%)
    reduce_scatter x1, waiting for transfers between devices, on_device(): cols = lax.psum_scatter(cols, 'ga', scatter_dimension=0, tiled=True)  85.2 us
    reduce_scatter x1, waiting for transfers between devices, on_device(): lax.psum_scatter(direct, 'pair', scatter_dimension=0, tiled=True)[0]  70.6 us
    all_gather x1, waiting for transfers between devices, on_device(): whole_con = lax.all_gather(con_density, 'ga', axis=0, tiled=True)  66.7 us
    all_gather x1, waiting for transfers between devices, on_device(): whole_val = lax.all_gather(val_density, 'pair', axis=0, tiled=True)  62.1 us
    all_gather x1, blocking collectives, on_device(): whole_here = lax.all_gather(trans_here, 'pair', axis=0, tiled=True)  26.4 us
    dot_general x10, matrix products, mul(): return jnp.einsum(spec, left, right, preferred_element_type=F32)  19.7 us
    all_to_all x1, blocking collectives, on_device(): lax.all_to_all(rows.reshape(pairs, NT // pairs, points, 2, NC), 'pair', s...  13.5 us
  transfers between devices with their start and end apart: 4, of which 4 were waited for; matrix products, arithmetic and copies ran while one was open for 5% of the time, Pallas kernels for 0%

commit v1 on v0

--- a/solution.py
+++ b/solution.py
@@ -24,7 +24,10 @@
     blocks = slab_cols // GBLK
     pairs = lax.axis_size("pair")
     slabs = lax.axis_size("ga")
-    whole_con = lax.all_gather(con_density, "ga", axis=0, tiled=True)
+    peers = lax.axis_size("ga")
+    pieces = jnp.stack([con_density for _ in range(peers)])
+    pieces = lax.all_to_all(pieces, "ga", split_axis=0, concat_axis=0)
+    whole_con = jnp.concatenate(pieces, axis=0)
     whole_val = lax.all_gather(val_density, "pair", axis=0, tiled=True)
     whole_here = lax.all_gather(trans_here, "pair", axis=0, tiled=True)
     within = (shift_map % GBLK).reshape(points, blocks, GBLK)

time: 405 us -> 388 us (0.958)
  waiting for transfers between devices: 285 us -> 236 us
  local copies, waits for them, and re-layouts: 39.7 us -> 51.6 us
  matrix products: 21.6 us -> 31 us
  starting transfers between devices: 0.12 us -> 9.07 us
    all_gather x1 -> x0, waiting for transfers between devices: 66.7 us -> none  [on_device(): whole_con = lax.all_gather(con_density, 'ga', axis=0, tiled=True)]
    all_gather x1, waiting for transfers between devices: 62.1 us -> 75.5 us  [on_device(): whole_val = lax.all_gather(val_density, 'pair', axis=0, tiled=True)]
    dot_general x10, matrix products: 19.7 us -> 29 us  [mul(): return jnp.einsum(spec, left, right, preferred_element_type=F32)]
    all_to_all x0 -> x1, starting transfers between devices: none -> 8.77 us  [on_device(): pieces = lax.all_to_all(pieces, 'ga', split_axis=0, concat_axis=0)]
    reshape x4, local copies, waits for them, and re-layouts: 4.09 us -> 9.29 us  [unshift(): return moved.reshape(points, NV * NV, slab_cols)]
    reduce_scatter x1, waiting for transfers between devices: 70.6 us -> 75.1 us  [on_device(): lax.psum_scatter(direct, 'pair', scatter_dimension=0, tiled=True)[0]]
    unnamed x37 -> x34, local copies, waits for them, and re-layouts: 5.97 us -> 8.96 us
  transfers between devices with their start and end apart: 4 -> 4, of which waited for: 4 -> 3; matrix products, arithmetic and copies ran while one was open for 5% -> 9% of each run, Pallas kernels for 0% -> 0%
where the time goes in v1:
time: 388 us; the launch traced here: 387 us
  waiting for transfers between devices  236 us (61%)
  local copies, waits for them, and re-layouts  51.6 us (13%)
  blocking collectives  40.1 us (10%)
  matrix products  31 us (8%)
  between operations  13.4 us (3%)
  starting transfers between devices  9.07 us (2%)
  other arithmetic  5.81 us (1%)
    reduce_scatter x1, waiting for transfers between devices, on_device(): cols = lax.psum_scatter(cols, 'ga', scatter_dimension=0, tiled=True)  85.4 us
    all_gather x1, waiting for transfers between devices, on_device(): whole_val = lax.all_gather(val_density, 'pair', axis=0, tiled=True)  75.5 us
    reduce_scatter x1, waiting for transfers between devices, on_device(): lax.psum_scatter(direct, 'pair', scatter_dimension=0, tiled=True)[0]  75.1 us
    dot_general x10, matrix products, mul(): return jnp.einsum(spec, left, right, preferred_element_type=F32)  29 us
    all_gather x1, blocking collectives, on_device(): whole_here = lax.all_gather(trans_here, 'pair', axis=0, tiled=True)  26.6 us
    all_to_all x1, blocking collectives, on_device(): lax.all_to_all(rows.reshape(pairs, NT // pairs, points, 2, NC), 'pair', s...  13.5 us
    reshape x4, local copies, waits for them, and re-layouts, unshift(): return moved.reshape(points, NV * NV, slab_cols)  9.29 us
    unnamed x34, local copies, waits for them, and re-layouts  8.96 us
  transfers between devices with their start and end apart: 4, of which 3 were waited for; matrix products, arithmetic and copies ran while one was open for 9% of the time, Pallas kernels for 0%

profile of v1, /device:TPU:2, one launch (start us, length us, event | category | flops | bytes accessed | tf_op | source)
XLA Modules:
  0.0 387.1 jit_solution(17503753351443991228)
XLA Ops:
  6.5 1.1 copy.95
  7.6 3.6 stack.17
  11.2 8.8 %all-to-all-start = ((bf16[16,36,3,2,512]{4,3,1,2,0:T(2,128)(2,1)}), bf16[16,36,3,2,512]{4,3,1,2,0:T(2,128)(2,1)S(1)}, u32[]{:S(2)}, u32[]{:S(2)}) async-start(bf16[16,36,3,2,512]{4,3,1,2,0:T(2,128)(2,1)} %stack.17), calls=%async_computation | async-start | bytes 7077888 | tf_op jit(solution)/shard_map/all_to_all | solution.py:29
  20.0 0.0 all-gather.2.cloned.1.call-start
  20.0 1.6 copy.84
  21.6 0.0 all-gather.2.cloned.1.call-update
  21.6 0.2 reduce-scatter.3.cloned.1.call-start
  21.8 0.0 copy-done.12
  21.9 75.5 %all-gather.2.cloned.1.call-done = bf16[256,3,2,512]{3,0,1,2:T(8,128)(2,1)} async-done(((bf16[16,3,2,512]{3,0,1,2:T(8,128)(2,1)}), bf16[256,3,2,512]{3,0,1,2:T(8,128)(2,1)}) %all-gather.2.cloned.1.call-update) | async-done | bytes 1572880 | tf_op jit(solution)/shard_map/all_gather | solution.py:31
  97.4 2.4 fusion.22
  99.8 0.2 copy-done
  100.0 2.7 fusion.42
  102.7 1.3 convolution_convert_fusion.1
  103.9 2.3 copy.94
  106.2 2.4 fusion.20
  108.6 0.2 copy-done.1
  108.8 2.6 fusion.43
  111.5 1.3 convolution_convert_fusion
  112.7 2.4 copy.92
  115.1 2.4 convolution_convert_fusion.3
  117.5 2.3 copy.93
  119.8 2.4 convolution_convert_fusion.2
  122.2 2.3 copy.89
  124.5 2.1 neg.7
  126.7 2.2 neg.6
  128.8 0.0 all-to-all-done
  128.8 2.4 copy.96
  131.3 4.2 %copy.97 = bf16[3,576,2,512]{3,2,1,0:T(2,128)(2,1)} copy(bf16[3,576,2,512]{3,2,0,1:T(2,128)(2,1)S(1)} %bitcast.117) | data formatting | bytes 7077888 | tf_op jit(solution)/shard_map/transpose | solution.py:57
  135.4 7.8 %reshape.60 = bf16[3,576,1024]{2,1,0:T(8,128)(2,1)S(1)} reshape(bf16[3,576,2,512]{3,2,1,0:T(2,128)(2,1)} %copy.97) | data formatting | bytes 7077888 | tf_op jit(solution)/shard_map/reshape | solution.py:57
  143.3 0.5 constant_dynamic-update-slice_fusion.1
  143.8 0.5 constant_dynamic-update-slice_fusion
  144.3 0.0 copy-start.4
  144.3 2.9 copy-done.4
  147.2 6.3 %fusion.8 = f32[3,256,576]{2,1,0:T(8,128)S(1)} fusion(bf16[3,576,2048]{2,1,0:T(8,128)(2,1)S(1)} %constant_dynamic-update-slice_fusion, bf16[3,256,512]{2,1,0:T(8,128)(2,1)} %copy.94, bf16[3,256,512]{2,1,0:T(8,128)(2,1)S(1)} %copy-done.2, bf16[3,256,512]{2,1,0:T(8,128)(2,1)} %copy.93, bf16[3,256,512]{2,1,0:T(8,128)(2,1)S(1)} %copy-done.3), kind=kOutput, calls=%fused_computation.11 | convolution fusion | flops 1824522240 | bytes 11993088 | tf_op jit(solution)/shard_map/kax,kbx->kab/dot_general | solution.py:39
  153.6 5.4 %fusion = f32[3,256,576]{2,1,0:T(8,128)S(1)} fusion(bf16[3,576,2048]{2,1,0:T(8,128)(2,1)} %copy-done.4, bf16[3,256,512]{2,1,0:T(8,128)(2,1)S(1)} %copy-done.7, bf16[3,256,512]{2,1,0:T(8,128)(2,1)S(1)} %copy-done.5, bf16[3,256,512]{2,1,0:T(8,128)(2,1)S(1)} %copy-done.8, bf16[3,256,512]{2,1,0:T(8,128)(2,1)S(1)} %copy-done.6), kind=kOutput, calls=%fused_computation.3 | convolution fusion | flops 1824522240 | bytes 11993088 | tf_op jit(solution)/shard_map/kax,kbx->kab/dot_general | solution.py:39
  159.0 0.3 maximum_bitcast_fusion
  159.3 3.1 copy.104
  162.3 0.0 reduce-scatter.3.cloned.1.call-update
  162.4 0.0 reduce-scatter.5.cloned.1.call-start
  162.4 0.7 copy-done.10
  163.2 0.1 copy-done.9
  163.3 26.6 %all_gather.6 = bf16[384,2,512]{2,0,1:T(8,128)(2,1)S(1)} all-gather(bf16[24,2,512]{2,0,1:T(8,128)(2,1)S(1)} %copy.83), channel_id=1, replica_groups=mesh['ga'=16,'pair'=16] {'pair'}, dimensions={0}, use_global_device_ids=true | all-gather | bytes 835584 | tf_op jit(solution)/shard_map/all_gather | solution.py:32
  190.0 0.5 fusion.56
  190.4 0.5 fusion.38
  190.9 0.5 fusion.57
  191.4 0.5 fusion.39
  191.9 75.1 %reduce-scatter.3.cloned.1.call-done = f32[1,3,2,16,576]{4,3,2,1,0:T(8,128)} async-done(((f32[16,3,2,16,576]{4,3,2,1,0:T(8,128)}), f32[1,3,2,16,576]{4,3,2,1,0:T(8,128)}) %reduce-scatter.3.cloned.1.call-update) | async-done | bytes 221200 | tf_op jit(solution)/shard_map/reduce_scatter | solution.py:63
  267.0 1.4 reshape_squeeze.3
  268.4 0.3 copy.113
  268.8 0.8 copy.106
  269.6 3.3 gather_fusion
  273.0 0.1 copy.141
  273.1 0.9 reshape.86
  274.0 13.5 %all_to_all.10 = f32[16,1,3456]{2,1,0:T(1,128)S(1)} all-to-all(f32[16,1,3456]{2,1,0:T(1,128)S(1)} %reshape.86), channel_id=1, replica_groups=mesh['ga'=16,'pair'=16] {'pair'}, dimensions={0} | all-to-all | bytes 442368 | tf_op jit(solution)/shard_map/all_to_all | solution.py:78
  287.4 0.5 broadcast.27
  288.0 1.2 reduce
  289.1 0.7 reshape.87
  289.8 0.1 bitcast_bitcast_fusion
  289.9 0.8 copy.114
  290.8 0.7 reshape.85
  291.5 2.2 gather_fusion.1
  293.7 0.0 reduce-scatter.5.cloned.1.call-update
  293.7 85.4 %reduce-scatter.5.cloned.1.call-done = f32[24,144]{1,0:T(8,128)} async-done(((f32[384,144]{1,0:T(8,128)}), f32[24,144]{1,0:T(8,128)}) %reduce-scatter.5.cloned.1.call-update) | async-done | bytes 13840 | tf_op jit(solution)/shard_map/reduce_scatter | solution.py:83
  379.1 1.5 copy.115
  (28 shorter events, 0.1 us)
Async XLA Ops:
  11.2 10.6 %copy-start.12 = (s32[3,512]{1,0:T(4,128)S(1)}, s32[3,512]{1,0:T(4,128)}, u32[]{:S(2)}) copy-start(s32[3,512]{1,0:T(4,128)} %param.14) | copy-start | bytes 18436
  11.2 117.6 %all-to-all-start = ((bf16[16,36,3,2,512]{4,3,1,2,0:T(2,128)(2,1)}), bf16[16,36,3,2,512]{4,3,1,2,0:T(2,128)(2,1)S(1)}, u32[]{:S(2)}, u32[]{:S(2)}) async-start(bf16[16,36,3,2,512]{4,3,1,2,0:T(2,128)(2,1)} %stack.17), calls=%async_computation | async-start | bytes 7077888 | tf_op jit(solution)/shard_map/all_to_all | solution.py:29
  20.0 77.4 %all-gather.2.cloned.1.call-start = ((), (), s32[]{:S(2)}) async-start(), calls=%async_computation.4 | async-start | bytes 1671168 | tf_op jit(solution)/shard_map/all_gather | solution.py:31
  21.6 245.4 %reduce-scatter.3.cloned.1.call-start = ((), (), s32[]{:S(2)}) async-start(), calls=%async_computation.5 | async-start | bytes 4177920 | tf_op jit(solution)/shard_map/reduce_scatter | solution.py:63
  97.4 2.6 copy-start
  106.2 2.6 copy-start.1
  143.8 3.4 copy-start.2
  143.8 3.4 copy-start.3
  144.3 2.9 copy-start.4
  147.2 6.4 %copy-start.5 = (bf16[3,256,512]{2,1,0:T(8,128)(2,1)S(1)}, bf16[3,256,512]{2,1,0:T(8,128)(2,1)}, u32[]{:S(2)}) copy-start(bf16[3,256,512]{2,1,0:T(8,128)(2,1)} %copy.94) | copy-start | bytes 2359300
  147.2 6.4 %copy-start.6 = (bf16[3,256,512]{2,1,0:T(8,128)(2,1)S(1)}, bf16[3,256,512]{2,1,0:T(8,128)(2,1)}, u32[]{:S(2)}) copy-start(bf16[3,256,512]{2,1,0:T(8,128)(2,1)} %copy.93) | copy-start | bytes 2359300
  147.2 6.4 %copy-start.7 = (bf16[3,256,512]{2,1,0:T(8,128)(2,1)S(1)}, bf16[3,256,512]{2,1,0:T(8,128)(2,1)}, u32[]{:S(2)}) copy-start(bf16[3,256,512]{2,1,0:T(8,128)(2,1)} %neg.7) | copy-start | bytes 2359300
  147.2 6.4 %copy-start.8 = (bf16[3,256,512]{2,1,0:T(8,128)(2,1)S(1)}, bf16[3,256,512]{2,1,0:T(8,128)(2,1)}, u32[]{:S(2)}) copy-start(bf16[3,256,512]{2,1,0:T(8,128)(2,1)} %neg.6) | copy-start | bytes 2359300
  162.3 0.8 copy-start.10
  162.3 0.8 copy-start.13
  162.3 1.0 copy-start.9
  162.3 1.0 copy-start.11
  162.4 216.8 %reduce-scatter.5.cloned.1.call-start = ((), (), s32[]{:S(2)}) async-start(), calls=%async_computation.6 | async-start | bytes 417792 | tf_op jit(solution)/shard_map/reduce_scatter | solution.py:83
Sparse Core Ops, SparseCore 0:
  23.6 73.7 all-gather.1
  162.5 104.4 reduce-scatter.2
  293.8 85.2 reduce-scatter.4
